TPU v7x, 128 devices: a whole 4x4x4 slice. The times are simulated.
128 devices in a mesh: vessel: 8 (over z, core), tissue: 16 (over y, x).
Axes of the slice: x: 4, y: 4, z: 4, core: 2. Of those that a mesh axis runs over, the one named last changes fastest.
Arguments:
- tissue_start: float32 [3, 32, 128, 128], P(None, 'vessel', 'tissue'), may hold values from 0 to 1
- consumption: float32 [3, 32, 128, 128], P(None, 'vessel', 'tissue'), may hold values from 0.002 to 0.05
- inlet: float32 [3, 512], P(None, ('vessel', 'tissue')), may hold values from 0.5 to 2
- flow: float32 [512, 256], P(('vessel', 'tissue')), may hold values from 0.3 to 30
- permeability: float32 [3], replicated, may hold values from 0.3 to 3
- intersection_count: int32 [512, 16], P(('vessel', 'tissue')), may hold values from 64 to 128, as said below
- intersection_segment: int32 [512, 16, 128], P(('vessel', 'tissue')), may hold values from 0 to 255
- intersection_voxel: int32 [512, 16, 128], P(('vessel', 'tissue')), may hold values from 0 to 4095
- intersection_weight: float32 [512, 16, 128], P(('vessel', 'tissue')), may hold values from 0.1 to 1
- upstream: int32 [512], P(('vessel', 'tissue')), may hold values from 0 to 511
Outputs:
- tissue_field: float32 [3, 32, 128, 128], P(None, 'vessel', 'tissue')
- vessel_field: float32 [3, 512, 256], P(None, ('vessel', 'tissue'))
Inputs may be any that keep to these rules, and one draw needn't show every extreme that they name: `intersection_count`: every block has all 128 slots live toward at least one tissue brick of its vessel part, at most 128 toward any, and at least 64 toward every other.
All inputs are finite; a program needn't handle non-finite values.
Results may differ from a plain program's by a relative error of at most 0.0001.
Values sent between devices are 32-bit elements; how exact they have to be, the bound alone decides.
No kernel may reach another device: no remote copies, remote signals or barrier semaphores. Data moves between devices by JAX's collectives and lax.ppermute only.
A program may use at most 128 MiB of HBM per device.

v0:
```python
import jax
import jax.numpy as jnp
from jax import lax
from jax.sharding import PartitionSpec as P

SEG = 256
OUTER = 2
SWEEPS = 4
DIFFUSION = (1.0, 0.7, 0.7)


def with_halo(value, sides, width):
    for axis, dim in sides:
        size, length = (lax.axis_size(axis), value.shape[dim])
        up = [(i, (i + 1) % size) for i in range(size - 1)]
        down = [(j, i) for i, j in up]
        last = lax.slice_in_dim(value, length - width, length, axis=dim)
        first = lax.slice_in_dim(value, 0, width, axis=dim)
        before = lax.ppermute(last, axis, up)
        after = lax.ppermute(first, axis, down)
        value = jnp.concatenate([before, value, after], axis=dim)
    return value


def combine(earlier, later):
    return (earlier[0] * later[0], later[0] * earlier[1] + later[1])


def relax_sweep(tissue, source, consumption):
    padded = with_halo(tissue, (("vessel", 1), ("tissue", 2)), 1)
    padded = jnp.pad(padded, ((0, 0), (0, 0), (0, 0), (1, 1)))
    neighbours = padded[:, 2:, 1:-1, 1:-1] + padded[:, :-2, 1:-1, 1:-1]
    neighbours = neighbours + padded[:, 1:-1, 2:, 1:-1] + padded[:, 1:-1, :-2, 1:-1]
    neighbours = neighbours + padded[:, 1:-1, 1:-1, 2:] + padded[:, 1:-1, 1:-1, :-2]
    rates = jnp.array(DIFFUSION, jnp.float32)[:, None, None, None]
    produced = jnp.zeros_like(tissue).at[2].set(2.0 * consumption[1] * tissue[1])
    return (source + produced + rates * neighbours) / (6.0 * rates + consumption)


def solve_blocks(arranged, flat_weight, flat_segment, flow, inflow_rows, permeability):

    def solve_block(block_items):
        slot_values, weight, segment, speed, inflow_row = block_items
        onehot = (segment[:, None] == jnp.arange(SEG)[None, :]).astype(jnp.float32)
        weight_sum = jnp.dot(weight, onehot, precision=lax.Precision.HIGHEST)
        gathered = jnp.dot(slot_values * weight[None, :], onehot, precision=lax.Precision.HIGHEST)
        denominator = speed[None, :] + permeability[:, None] * weight_sum[None, :]
        decay_rate = speed[None, :] / denominator
        drive_term = permeability[:, None] * gathered / denominator
        drive_term = drive_term.at[:, 0].add(decay_rate[:, 0] * inflow_row)
        _, vessel = lax.associative_scan(combine, (decay_rate, drive_term), axis=1)
        at_slot = jnp.dot(vessel, onehot.T, precision=lax.Precision.HIGHEST)
        slot_flux = permeability[:, None] * weight[None, :] * (at_slot - slot_values)
        return (vessel, slot_flux)

    return lax.map(solve_block, (arranged, flat_weight, flat_segment, flow, inflow_rows))


def shards(
    tissue_start,
    consumption,
    inlet,
    flow,
    permeability,
    intersection_count,
    intersection_segment,
    intersection_voxel,
    intersection_weight,
    upstream,
):
    blocks_here, columns, slots = intersection_voxel.shape
    species, depth, rows_here, width = tissue_start.shape
    voxels = depth * rows_here * width
    live_slot = jnp.arange(slots)[None, None, :] < intersection_count[:, :, None]
    weight = jnp.where(live_slot, intersection_weight, 0.0)
    flat_weight = weight.reshape(blocks_here, -1)
    flat_segment = intersection_segment.reshape(blocks_here, -1)
    full_rows = rows_here * columns
    column = jnp.arange(columns)[None, :, None]
    region_index = (
        intersection_voxel // (rows_here * width) * full_rows
        + column * rows_here
        + intersection_voxel // width % rows_here
    ) * width + intersection_voxel % width
    region_index = region_index.reshape(-1)
    tissue = tissue_start
    inflow_rows = inlet.T
    vessel = jnp.zeros((blocks_here, species, SEG), jnp.float32)
    for outer_step in range(OUTER):
        region = lax.all_gather(tissue, "tissue", axis=2, tiled=True).reshape(species, -1)
        slot_values = region[:, region_index].reshape(species, blocks_here, columns, slots)
        arranged = jnp.swapaxes(slot_values, 0, 1).reshape(blocks_here, species, -1)
        vessel, slot_flux = solve_blocks(
            arranged, flat_weight, flat_segment, flow, inflow_rows, permeability
        )
        gathered_ends = lax.all_gather(
            vessel[:, :, SEG - 1], ("vessel", "tissue"), axis=0, tiled=True
        )
        inflow_rows = 0.5 * (inlet.T + gathered_ends[upstream])
        flux_grid = jnp.swapaxes(slot_flux.reshape(blocks_here, species, columns, slots), 0, 1)
        partial_source = jax.vmap(
            lambda species_row: jax.ops.segment_sum(species_row, region_index, voxels * columns)
        )(flux_grid.reshape(species, -1))
        source = lax.psum_scatter(
            partial_source.reshape(species, depth, full_rows, width),
            "tissue",
            scatter_dimension=2,
            tiled=True,
        )
        for sweep_step in range(SWEEPS):
            tissue = relax_sweep(tissue, source, consumption)
    return (tissue, jnp.swapaxes(vessel, 0, 1))


def solution(mesh):
    return jax.shard_map(
        shards,
        mesh=mesh,
        in_specs=(
            P(None, "vessel", "tissue", None),
            P(None, "vessel", "tissue", None),
            P(None, ("vessel", "tissue")),
            P(("vessel", "tissue"), None),
            P(),
            P(("vessel", "tissue"), None),
            P(("vessel", "tissue"), None, None),
            P(("vessel", "tissue"), None, None),
            P(("vessel", "tissue"), None, None),
            P(("vessel", "tissue")),
        ),
        out_specs=(P(None, "vessel", "tissue", None), P(None, ("vessel", "tissue"), None)),
        check_vma=False,
    )
```

profile of v0, /device:TPU:40, one launch (start us, length us, event | category | flops | bytes accessed | tf_op | source)
XLA Modules:
  0.0 754.9 jit_solution(14316864906050526464)
XLA Ops:
  7.2 25.3 %all_gather.9 = f32[3,4,128,128]{3,2,1,0:T(8,128)S(1)} all-gather(f32[3,4,8,128]{3,2,1,0:T(8,128)} %param.42), channel_id=1, replica_groups=mesh['vessel'=8,'tissue'=16] {'tissue'}, dimensions={2}, use_global_device_ids=true | all-gather | bytes 835584 | tf_op jit(solution)/shard_map/all_gather | solution.py:90
  32.5 16.6 %copy.52 = f32[3,4,128,128]{0,3,2,1:T(8,128)} copy(f32[3,4,128,128]{3,2,1,0:T(8,128)S(1)} %all_gather.9) | data formatting | bytes 1572864 | tf_op jit(solution)/shard_map/all_gather | solution.py:90
  49.3 38.3 %gather_fusion = f32[8192,3]{1,0:T(8,128)} fusion(f32[3,65536]{0,1:T(8,128)} %bitcast.162, s32[8192]{0:T(1024)S(1)} %broadcast_clamp_fusion), kind=kCustom, calls=%fused_computation | custom fusion | bytes 229376 | tf_op jit(solution)/shard_map/gather | solution.py:91
  90.8 48.8 %while.38 = (s32[]{:T(128)}, f32[4,3,256]{2,1,0:T(4,128)S(1)}, f32[4,3,2048]{2,1,0:T(4,128)S(1)}, f32[3]{0:T(128)S(1)}, f32[4,3,2048]{2,0,1:T(4,128)S(1)}, /*ind...) while((s32[]{:T(128)}, f32[4,3,256]{2,1,0:T(4,128)S(1)}, ...), condition=%wide.region_2.3_spmd, body=%wide.region_0.2_spmd.sunk | while | flops 45649856 | bytes 347579 | solution.py:56
  142.4 57.5 %scatter_custom_fusion = f32[3,65536]{0,1:T(8,128)} fusion(s32[8192]{0:T(1024)S(1)} %bitcast.196, f32[8192,3]{1,0:T(8,128)} %bitcast.167, f32[]{:T(128)} %constant.353.clone.1), kind=kCustom, calls=%fused_computation.111 | custom fusion | flops 24576 | bytes 786944 | tf_op jit(solution)/shard_map/vmap()/scatter-add | solution.py:102
  199.9 20.3 %copy.58 = f32[3,4,128,128]{3,2,1,0:T(8,128)} copy(f32[3,4,128,128]{0,3,2,1:T(8,128)} %bitcast.161) | data formatting | bytes 1572864 | tf_op jit(solution)/shard_map/reshape | solution.py:105
  227.3 4.5 collective-permute-start.2
  233.7 5.8 collective-permute-done.3
  239.7 53.1 %reduce-scatter.3.cloned.1.call-done = f32[3,4,8,128]{3,2,1,0:T(8,128)} async-done(((f32[3,4,128,128]{3,2,1,0:T(8,128)}), f32[3,4,8,128]{3,2,1,0:T(8,128)}) %reduce-scatter.3.cloned.1.call-update) | async-done | bytes 49168 | tf_op jit(solution)/shard_map/reduce_scatter | solution.py:104
  304.4 4.6 collective-permute-start.6
  311.0 5.7 collective-permute-done.7
  321.6 55.9 %all-gather = f32[512,3,1]{1,2,0:T(1,128)S(1)} all-gather(f32[4,3,1]{1,2,0:T(1,128)S(1)} %slice.1438), channel_id=2, replica_groups=mesh['vessel'=8,'tissue'=16] {'vessel','tissue'}, dimensions={0}, use_global_device_ids=true | all-gather | bytes 6192 | tf_op jit(solution)/shard_map/all_gather | solution.py:96
  384.0 5.2 collective-permute-done.11
  408.3 23.5 %all_gather.10 = f32[3,4,128,128]{3,2,1,0:T(8,128)S(1)} all-gather(f32[3,4,8,128]{3,2,1,0:T(8,128)S(1)} %fusion.65), channel_id=1, replica_groups=mesh['vessel'=8,'tissue'=16] {'tissue'}, dimensions={2}, use_global_device_ids=true | all-gather | bytes 835584 | tf_op jit(solution)/shard_map/all_gather | solution.py:90
  431.8 16.6 %copy.59 = f32[3,4,128,128]{0,3,2,1:T(8,128)} copy(f32[3,4,128,128]{3,2,1,0:T(8,128)S(1)} %all_gather.10) | data formatting | bytes 1572864 | tf_op jit(solution)/shard_map/all_gather | solution.py:90
  448.4 38.3 %gather_fusion.1 = f32[8192,3]{1,0:T(8,128)} fusion(f32[3,65536]{0,1:T(8,128)} %bitcast.163, s32[8192]{0:T(1024)S(1)} %broadcast_clamp_fusion), kind=kCustom, calls=%fused_computation.1 | custom fusion | bytes 229376 | tf_op jit(solution)/shard_map/gather | solution.py:91
  489.5 49.1 %while.39 = (s32[]{:T(128)}, f32[4,3,256]{2,0,1:T(4,128)S(1)}, f32[4,3,2048]{2,1,0:T(4,128)S(1)}, f32[3]{0:T(128)S(1)}, f32[4,3,2048]{2,0,1:T(4,128)S(1)}, /*ind...) while((s32[]{:T(128)}, f32[4,3,256]{2,0,1:T(4,128)S(1)}, ...), condition=%wide.region_7.8_spmd, body=%wide.region_5.7_spmd.sunk | while | flops 45649856 | bytes 356795 | solution.py:56
  541.5 57.5 %scatter_custom_fusion.1 = f32[3,65536]{0,1:T(8,128)} fusion(s32[8192]{0:T(1024)S(1)} %bitcast.197, f32[8192,3]{1,0:T(8,128)} %bitcast.166, f32[]{:T(128)} %constant.353.clone.1), kind=kCustom, calls=%fused_computation.109 | custom fusion | flops 24576 | bytes 786944 | tf_op jit(solution)/shard_map/vmap()/scatter-add | solution.py:102
  599.0 20.2 %copy.65 = f32[3,4,128,128]{3,2,1,0:T(8,128)} copy(f32[3,4,128,128]{0,3,2,1:T(8,128)} %bitcast.160) | data formatting | bytes 1572864 | tf_op jit(solution)/shard_map/reshape | solution.py:105
  626.2 4.6 collective-permute-start.18
  632.7 5.7 collective-permute-done.19
  638.7 50.8 %reduce-scatter.5.cloned.1.call-done = f32[3,4,8,128]{3,2,1,0:T(8,128)} async-done(((f32[3,4,128,128]{3,2,1,0:T(8,128)}), f32[3,4,8,128]{3,2,1,0:T(8,128)}) %reduce-scatter.5.cloned.1.call-update) | async-done | bytes 49168 | tf_op jit(solution)/shard_map/reduce_scatter | solution.py:104
  701.1 4.6 collective-permute-start.22
  707.6 5.7 collective-permute-done.23
  (944 shorter events, 218.0 us)
Async XLA Ops:
  7.2 285.7 %reduce-scatter.3.cloned.1.call-start = ((), (), s32[]{:S(2)}) async-start(), calls=%async_computation.2 | async-start | bytes 835584 | tf_op jit(solution)/shard_map/reduce_scatter | solution.py:104
  220.2 469.3 %reduce-scatter.5.cloned.1.call-start = ((), (), s32[]{:S(2)}) async-start(), calls=%async_computation.3 | async-start | bytes 835584 | tf_op jit(solution)/shard_map/reduce_scatter | solution.py:104
  220.3 5.6 collective-permute-start.1
  222.2 5.0 collective-permute-start
  227.3 6.4 collective-permute-start.2
  231.8 7.7 %collective-permute-start.3 = (f32[3,6,1,128]{3,2,1,0:T(1,128)S(1)}, f32[3,6,1,128]{3,2,1,0:T(1,128)S(1)}, u32[]{:S(2)}, u32[]{:S(2)}) collective-permute-start(f32[3,6,1,128]{3,2,1,0:T(1,128)S(1)} %get-tuple-element.476), channel_id=1, source_target_pairs={{0,1},{1,2},{2,3},{3,4},{4,5},{5,6},{6,7},{7,8},{8,9},{9,10},{10,1... | collective-permute-start | bytes 27656 | tf_op jit(solution)/shard_map/ppermute | solution.py:19
  299.4 5.0 collective-permute-start.5
  304.4 6.5 collective-permute-start.6
  309.0 7.7 %collective-permute-start.7 = (f32[3,6,1,128]{3,2,1,0:T(1,128)S(1)}, f32[3,6,1,128]{3,2,1,0:T(1,128)S(1)}, u32[]{:S(2)}, u32[]{:S(2)}) collective-permute-start(f32[3,6,1,128]{3,2,1,0:T(1,128)S(1)} %get-tuple-element.474), channel_id=1, source_target_pairs={{0,1},{1,2},{2,3},{3,4},{4,5},{5,6},{6,7},{7,8},{8,9},{9,10},{10,1... | collective-permute-start | bytes 27656 | tf_op jit(solution)/shard_map/ppermute | solution.py:19
  317.0 61.0 %collective-permute-start.8 = (f32[3,1,8,128]{3,2,1,0:T(8,128)S(1)}, f32[3,1,8,128]{3,2,1,0:T(8,128)S(1)}, u32[]{:S(2)}, u32[]{:S(2)}) collective-permute-start(f32[3,1,8,128]{3,2,1,0:T(8,128)S(1)} %get-tuple-element.489), channel_id=1, source_target_pairs={{16,0},{32,16},{48,32},{64,48},{80,64},{96,80},{112,96},{17,1},{33... | collective-permute-start | bytes 36872 | tf_op jit(solution)/shard_map/ppermute | solution.py:20
  318.9 59.1 %collective-permute-start.9 = (f32[3,1,8,128]{3,2,1,0:T(8,128)S(1)}, f32[3,1,8,128]{3,2,1,0:T(8,128)S(1)}, u32[]{:S(2)}, u32[]{:S(2)}) collective-permute-start(f32[3,1,8,128]{3,2,1,0:T(8,128)S(1)} %get-tuple-element.488), channel_id=1, source_target_pairs={{0,16},{16,32},{32,48},{48,64},{64,80},{80,96},{96,112},{1,17},{17... | collective-permute-start | bytes 36872 | tf_op jit(solution)/shard_map/ppermute | solution.py:19
  378.1 5.9 collective-permute-start.10
  381.5 7.7 %collective-permute-start.11 = (f32[3,6,1,128]{3,2,1,0:T(1,128)S(1)}, f32[3,6,1,128]{3,2,1,0:T(1,128)S(1)}, u32[]{:S(2)}, u32[]{:S(2)}) collective-permute-start(f32[3,6,1,128]{3,2,1,0:T(1,128)S(1)} %get-tuple-element.472), channel_id=1, source_target_pairs={{0,1},{1,2},{2,3},{3,4},{4,5},{5,6},{6,7},{7,8},{8,9},{9,10},{10,1... | collective-permute-start | bytes 27656 | tf_op jit(solution)/shard_map/ppermute | solution.py:19
  392.1 6.2 collective-permute-start.13
  398.3 5.9 collective-permute-start.14
  400.3 7.7 %collective-permute-start.15 = (f32[3,6,1,128]{3,2,1,0:T(1,128)S(1)}, f32[3,6,1,128]{3,2,1,0:T(1,128)S(1)}, u32[]{:S(2)}, u32[]{:S(2)}) collective-permute-start(f32[3,6,1,128]{3,2,1,0:T(1,128)S(1)} %get-tuple-element.470), channel_id=1, source_target_pairs={{0,1},{1,2},{2,3},{3,4},{4,5},{5,6},{6,7},{7,8},{8,9},{9,10},{10,1... | collective-permute-start | bytes 27656 | tf_op jit(solution)/shard_map/ppermute | solution.py:19
  626.2 6.5 collective-permute-start.18
  630.8 7.7 %collective-permute-start.19 = (f32[3,6,1,128]{3,2,1,0:T(1,128)S(1)}, f32[3,6,1,128]{3,2,1,0:T(1,128)S(1)}, u32[]{:S(2)}, u32[]{:S(2)}) collective-permute-start(f32[3,6,1,128]{3,2,1,0:T(1,128)S(1)} %get-tuple-element.468), channel_id=1, source_target_pairs={{0,1},{1,2},{2,3},{3,4},{4,5},{5,6},{6,7},{7,8},{8,9},{9,10},{10,1... | collective-permute-start | bytes 27656 | tf_op jit(solution)/shard_map/ppermute | solution.py:19
  701.1 6.6 collective-permute-start.22
  705.7 7.7 %collective-permute-start.23 = (f32[3,6,1,128]{3,2,1,0:T(1,128)S(1)}, f32[3,6,1,128]{3,2,1,0:T(1,128)S(1)}, u32[]{:S(2)}, u32[]{:S(2)}) collective-permute-start(f32[3,6,1,128]{3,2,1,0:T(1,128)S(1)} %get-tuple-element.466), channel_id=1, source_target_pairs={{0,1},{1,2},{2,3},{3,4},{4,5},{5,6},{6,7},{7,8},{8,9},{9,10},{10,1... | collective-permute-start | bytes 27656 | tf_op jit(solution)/shard_map/ppermute | solution.py:19
  720.6 5.9 collective-permute-start.26
  722.6 7.7 %collective-permute-start.27 = (f32[3,6,1,128]{3,2,1,0:T(1,128)S(1)}, f32[3,6,1,128]{3,2,1,0:T(1,128)S(1)}, u32[]{:S(2)}, u32[]{:S(2)}) collective-permute-start(f32[3,6,1,128]{3,2,1,0:T(1,128)S(1)} %get-tuple-element.464), channel_id=1, source_target_pairs={{0,1},{1,2},{2,3},{3,4},{4,5},{5,6},{6,7},{7,8},{8,9},{9,10},{10,1... | collective-permute-start | bytes 27656 | tf_op jit(solution)/shard_map/ppermute | solution.py:19
  737.5 5.9 collective-permute-start.30
  739.5 7.7 %collective-permute-start.31 = (f32[3,6,1,128]{3,2,1,0:T(1,128)S(1)}, f32[3,6,1,128]{3,2,1,0:T(1,128)S(1)}, u32[]{:S(2)}, u32[]{:S(2)}) collective-permute-start(f32[3,6,1,128]{3,2,1,0:T(1,128)S(1)} %get-tuple-element.462), channel_id=1, source_target_pairs={{0,1},{1,2},{2,3},{3,4},{4,5},{5,6},{6,7},{7,8},{8,9},{9,10},{10,1... | collective-permute-start | bytes 27656 | tf_op jit(solution)/shard_map/ppermute | solution.py:19
  (23 other events, 783.0 us)
Sparse Core Ops, SparseCore 0:
  220.3 72.4 reduce-scatter.2
  619.3 70.1 reduce-scatter.4
where the time goes:
time: 757 us; the launch traced here: 755 us
  local copies, waits for them, and re-layouts  224 us (30%)
  waiting for transfers between devices  162 us (21%)
  other arithmetic  141 us (19%)
  blocking collectives  105 us (14%)
  starting transfers between devices  85.4 us (11%)
  matrix products  21.3 us (3%)
  between operations  14.9 us (2%)
    scatter-add x2, other arithmetic, shards(): jax.ops.segment_sum(species_row, region_index, voxels * columns)  115 us
    reduce_scatter x2, waiting for transfers between devices, shards(): lax.psum_scatter(partial_source.reshape(species, depth, full_rows, width)...  104 us
    gather x2, local copies, waits for them, and re-layouts, shards(): region[:, region_index].reshape(species, blocks_here, columns, slots)  76.5 us
    ppermute x16, waiting for transfers between devices, with_halo(): before = lax.ppermute(last, axis, up)  56.4 us
    all_gather x1, blocking collectives, shards(): lax.all_gather(vessel[:, :, SEG - 1], ('vessel', 'tissue'), axis=0, tiled...  55.9 us
    all_gather x2, blocking collectives, shards(): lax.all_gather(tissue, 'tissue', axis=2, tiled=True).reshape(species, -1)  48.8 us
    ppermute x16, starting transfers between devices, with_halo(): after = lax.ppermute(first, axis, down)  45.2 us
    slice x320, local copies, waits for them, and re-layouts, solve_block(): _, vessel = lax.associative_scan(combine, (decay_rate, drive_term), axis=1)  41.6 us
  transfers between devices with their start and end apart: 34, of which 17 were waited for; matrix products, arithmetic and copies ran while one was open for 0% of the time, Pallas kernels for 0%

commit v1 on v0

--- a/solution.py
+++ b/solution.py
@@ -7,6 +7,27 @@
 OUTER = 2
 SWEEPS = 4
 DIFFUSION = (1.0, 0.7, 0.7)
+
+
+def gather_around(shard, axis, dim):
+    size, index, width = (lax.axis_size(axis), lax.axis_index(axis), shard.shape[dim])
+    ahead = [(i, (i + 1) % size) for i in range(size)]
+    left = [(i, (i - 1) % size) for i in range(size)]
+    result = jnp.zeros((*shard.shape[:dim], size * width, *shard.shape[dim + 1 :]), shard.dtype)
+    result = lax.dynamic_update_slice_in_dim(result, shard, index * width, axis=dim)
+    from_left = from_right = shard
+    halfway = size // 2
+    for step in range(1, halfway + 1):
+        from_left = lax.ppermute(from_left, axis, ahead)
+        result = lax.dynamic_update_slice_in_dim(
+            result, from_left, (index - step) % size * width, axis=dim
+        )
+        if step < size - halfway:
+            from_right = lax.ppermute(from_right, axis, left)
+            result = lax.dynamic_update_slice_in_dim(
+                result, from_right, (index + step) % size * width, axis=dim
+            )
+    return result
 
 
 def with_halo(value, sides, width):
@@ -87,7 +108,7 @@
     inflow_rows = inlet.T
     vessel = jnp.zeros((blocks_here, species, SEG), jnp.float32)
     for outer_step in range(OUTER):
-        region = lax.all_gather(tissue, "tissue", axis=2, tiled=True).reshape(species, -1)
+        region = gather_around(tissue, "tissue", 2).reshape(species, -1)
         slot_values = region[:, region_index].reshape(species, blocks_here, columns, slots)
         arranged = jnp.swapaxes(slot_values, 0, 1).reshape(blocks_here, species, -1)
         vessel, slot_flux = solve_blocks(

time: 757 us -> 865 us (1.14)
  local copies, waits for them, and re-layouts: 224 us -> 283 us
  starting transfers between devices: 85.4 us -> 143 us
  blocking collectives: 105 us -> 55.9 us
  waiting for transfers between devices: 162 us -> 178 us
  other arithmetic: 141 us -> 155 us
    ppermute x0 -> x30, starting transfers between devices: none -> 58.6 us  [the longest x14 56.4 us: gather_around(): from_right = lax.ppermute(from_right, axis, left)]
    dynamic_update_slice x0 -> x32, local copies, waits for them, and re-layouts: none -> 49 us  [the longest x16 24.5 us: gather_around(): lax.dynamic_update_slice_in_dim(result, from_left, (index - step) % size...]
    all_gather x2 -> x0, blocking collectives: 48.8 us -> none  [shards(): lax.all_gather(tissue, 'tissue', axis=2, tiled=True).reshape(species, -1)]
    all_gather x2 -> x0, local copies, waits for them, and re-layouts: 33.2 us -> none  [shards(): lax.all_gather(tissue, 'tissue', axis=2, tiled=True).reshape(species, -1)]
    another operation x2 -> x4, local copies, waits for them, and re-layouts: 0.04 us -> 22.6 us
    ppermute x0 -> x30, local copies, waits for them, and re-layouts: none -> 19 us  [the longest x16 10.1 us: gather_around(): from_left = lax.ppermute(from_left, axis, ahead)]
    scatter-add x2, other arithmetic: 115 us -> 128 us  [shards(): jax.ops.segment_sum(species_row, region_index, voxels * columns)]
    reduce_scatter x2, waiting for transfers between devices: 104 us -> 116 us  [shards(): lax.psum_scatter(partial_source.reshape(species, depth, full_rows, width)...]
  transfers between devices with their start and end apart: 34 -> 64, of which waited for: 17 -> 20; matrix products, arithmetic and copies ran while one was open for 0% -> 11% of each run, Pallas kernels for 0% -> 0%
where the time goes in v1:
time: 865 us; the launch traced here: 854 us
  local copies, waits for them, and re-layouts  283 us (33%)
  waiting for transfers between devices  178 us (21%)
  other arithmetic  155 us (18%)
  starting transfers between devices  143 us (17%)
  blocking collectives  55.9 us (6%)
  matrix products  21.3 us (2%)
  between operations  15.7 us (2%)
    scatter-add x2, other arithmetic, shards(): jax.ops.segment_sum(species_row, region_index, voxels * columns)  128 us
    reduce_scatter x2, waiting for transfers between devices, shards(): lax.psum_scatter(partial_source.reshape(species, depth, full_rows, width)...  116 us
    gather x2, local copies, waits for them, and re-layouts, shards(): region[:, region_index].reshape(species, blocks_here, columns, slots)  76.8 us
    ppermute x14, starting transfers between devices, gather_around(): from_right = lax.ppermute(from_right, axis, left)  56.4 us
    all_gather x1, blocking collectives, shards(): lax.all_gather(vessel[:, :, SEG - 1], ('vessel', 'tissue'), axis=0, tiled...  55.9 us
    ppermute x16, waiting for transfers between devices, with_halo(): before = lax.ppermute(last, axis, up)  52.6 us
    ppermute x16, starting transfers between devices, with_halo(): before = lax.ppermute(last, axis, up)  44 us
    slice x320, local copies, waits for them, and re-layouts, solve_block(): _, vessel = lax.associative_scan(combine, (decay_rate, drive_term), axis=1)  41.4 us
  transfers between devices with their start and end apart: 64, of which 20 were waited for; matrix products, arithmetic and copies ran while one was open for 11% of the time, Pallas kernels for 0%

profile of v1, /device:TPU:40, one launch (start us, length us, event | category | flops | bytes accessed | tf_op | source)
XLA Modules:
  0.0 854.3 jit_solution(14692155719659073340)
XLA Ops:
  14.6 11.3 %broadcast.401.clone = f32[3,4,128,128]{0,3,2,1:T(8,128)} broadcast(f32[]{:T(128)} %constant.468.clone.1), dimensions={} | broadcast | bytes 786436 | tf_op jit(solution)/shard_map/broadcast.27
  48.6 4.2 collective-permute-start.7
  74.1 4.2 collective-permute-start.13
  88.7 38.4 %gather_fusion = f32[8192,3]{1,0:T(8,128)} fusion(f32[3,65536]{0,1:T(8,128)} %bitcast.19, s32[8192]{0:T(1024)S(1)} %broadcast_clamp_fusion), kind=kCustom, calls=%fused_computation | custom fusion | bytes 229376 | tf_op jit(solution)/shard_map/gather | solution.py:112
  130.1 48.8 %while.38 = (s32[]{:T(128)}, f32[4,3,256]{2,1,0:T(4,128)S(1)}, f32[4,3,2048]{2,1,0:T(4,128)S(1)}, f32[3]{0:T(128)S(1)}, f32[4,3,2048]{2,0,1:T(4,128)S(1)}, /*ind...) while((s32[]{:T(128)}, f32[4,3,256]{2,1,0:T(4,128)S(1)}, ...), condition=%wide.region_2.3_spmd, body=%wide.region_0.2_spmd.sunk | while | flops 45649856 | bytes 347571 | solution.py:77
  181.6 70.0 %scatter_custom_fusion = f32[3,65536]{0,1:T(8,128)} fusion(s32[8192]{0:T(1024)S(1)} %bitcast.194, f32[8192,3]{1,0:T(8,128)} %bitcast.165, f32[]{:T(128)} %constant.468.clone.1), kind=kCustom, calls=%fused_computation.111 | custom fusion | flops 24576 | bytes 786944 | tf_op jit(solution)/shard_map/vmap()/scatter-add | solution.py:123
  251.7 20.2 %copy.133 = f32[3,4,128,128]{3,2,1,0:T(8,128)} copy(f32[3,4,128,128]{0,3,2,1:T(8,128)} %bitcast.161) | data formatting | bytes 1572864 | tf_op jit(solution)/shard_map/reshape | solution.py:126
  288.9 62.1 %reduce-scatter.3.cloned.1.call-done = f32[3,4,8,128]{3,2,1,0:T(8,128)} async-done(((f32[3,4,128,128]{3,2,1,0:T(8,128)}), f32[3,4,8,128]{3,2,1,0:T(8,128)}) %reduce-scatter.3.cloned.1.call-update) | async-done | bytes 49168 | tf_op jit(solution)/shard_map/reduce_scatter | solution.py:125
  362.6 4.6 collective-permute-start.21
  369.1 5.7 collective-permute-done.22
  379.8 55.9 %all-gather = f32[512,3,1]{1,2,0:T(1,128)S(1)} all-gather(f32[4,3,1]{1,2,0:T(1,128)S(1)} %slice.1438), channel_id=2, replica_groups=mesh['vessel'=8,'tissue'=16] {'vessel','tissue'}, dimensions={0}, use_global_device_ids=true | all-gather | bytes 6192 | tf_op jit(solution)/shard_map/all_gather | solution.py:117
  442.1 5.2 collective-permute-done.26
  452.2 4.2 collective-permute-done.28
  471.3 11.3 %broadcast.401 = f32[3,4,128,128]{0,3,2,1:T(8,128)} broadcast(f32[]{:T(128)} %constant.468.clone.1), dimensions={} | broadcast | bytes 786436 | tf_op jit(solution)/shard_map/broadcast.27
  505.6 4.2 collective-permute-start.38
  522.9 4.2 collective-permute-start.42
  531.7 4.2 collective-permute-start.44
  546.7 38.4 %gather_fusion.1 = f32[8192,3]{1,0:T(8,128)} fusion(f32[3,65536]{0,1:T(8,128)} %bitcast.30, s32[8192]{0:T(1024)S(1)} %broadcast_clamp_fusion), kind=kCustom, calls=%fused_computation.1 | custom fusion | bytes 229376 | tf_op jit(solution)/shard_map/gather | solution.py:112
  588.0 49.1 %while.39 = (s32[]{:T(128)}, f32[4,3,256]{2,0,1:T(4,128)S(1)}, f32[4,3,2048]{2,1,0:T(4,128)S(1)}, f32[3]{0:T(128)S(1)}, f32[4,3,2048]{2,0,1:T(4,128)S(1)}, /*ind...) while((s32[]{:T(128)}, f32[4,3,256]{2,0,1:T(4,128)S(1)}, ...), condition=%wide.region_7.8_spmd, body=%wide.region_5.7_spmd.sunk | while | flops 45649856 | bytes 356787 | solution.py:77
  639.9 57.7 %scatter_custom_fusion.1 = f32[3,65536]{0,1:T(8,128)} fusion(s32[8192]{0:T(1024)S(1)} %bitcast.195, f32[8192,3]{1,0:T(8,128)} %bitcast.164, f32[]{:T(128)} %constant.468.clone.1), kind=kCustom, calls=%fused_computation.109 | custom fusion | flops 24576 | bytes 786944 | tf_op jit(solution)/shard_map/vmap()/scatter-add | solution.py:123
  697.6 20.2 %copy.155 = f32[3,4,128,128]{3,2,1,0:T(8,128)} copy(f32[3,4,128,128]{0,3,2,1:T(8,128)} %bitcast.160) | data formatting | bytes 1572864 | tf_op jit(solution)/shard_map/reshape | solution.py:126
  734.8 53.7 %reduce-scatter.5.cloned.1.call-done = f32[3,4,8,128]{3,2,1,0:T(8,128)} async-done(((f32[3,4,128,128]{3,2,1,0:T(8,128)}), f32[3,4,8,128]{3,2,1,0:T(8,128)}) %reduce-scatter.5.cloned.1.call-update) | async-done | bytes 49168 | tf_op jit(solution)/shard_map/reduce_scatter | solution.py:125
  800.1 4.6 collective-permute-start.52
  806.6 5.7 collective-permute-done.53
  (1060 shorter events, 346.6 us)
Async XLA Ops:
  7.2 343.8 %reduce-scatter.3.cloned.1.call-start = ((), (), s32[]{:S(2)}) async-start(), calls=%async_computation.2 | async-start | bytes 835584 | tf_op jit(solution)/shard_map/reduce_scatter | solution.py:125
  7.2 20.3 %collective-permute-start = (f32[3,4,8,128]{3,2,1,0:T(8,128)}, f32[3,4,8,128]{3,2,1,0:T(8,128)S(1)}, u32[]{:S(2)}, u32[]{:S(2)}) collective-permute-start(f32[3,4,8,128]{3,2,1,0:T(8,128)} %param.42), channel_id=1, source_target_pairs={{0,1},{1,2},{2,3},{3,4},{4,5},{5,6},{6,7},{7,8},{8,9},{9,10},{10,1... | collective-permute-start | bytes 147464 | tf_op jit(solution)/shard_map/ppermute | solution.py:21
  8.8 20.9 %collective-permute-start.1 = (f32[3,4,8,128]{3,2,1,0:T(8,128)}, f32[3,4,8,128]{3,2,1,0:T(8,128)S(1)}, u32[]{:S(2)}, u32[]{:S(2)}) collective-permute-start(f32[3,4,8,128]{3,2,1,0:T(8,128)} %param.42), channel_id=1, source_target_pairs={{0,15},{1,0},{2,1},{3,2},{4,3},{5,4},{6,5},{7,6},{8,7},{9,8},{10,9... | collective-permute-start | bytes 147464 | tf_op jit(solution)/shard_map/ppermute | solution.py:26
  65.5 6.5 collective-permute-start.11
  71.7 6.6 collective-permute-start.12
  271.9 516.6 %reduce-scatter.5.cloned.1.call-start = ((), (), s32[]{:S(2)}) async-start(), calls=%async_computation.3 | async-start | bytes 835584 | tf_op jit(solution)/shard_map/reduce_scatter | solution.py:125
  281.0 7.7 collective-permute-start.18
  362.6 6.5 collective-permute-start.21
  367.2 7.7 collective-permute-start.22
  375.2 61.0 %collective-permute-start.23 = (f32[3,1,8,128]{3,2,1,0:T(8,128)S(1)}, f32[3,1,8,128]{3,2,1,0:T(8,128)S(1)}, u32[]{:S(2)}, u32[]{:S(2)}) collective-permute-start(f32[3,1,8,128]{3,2,1,0:T(8,128)S(1)} %get-tuple-element.489), channel_id=1, source_target_pairs={{16,0},{32,16},{48,32},{64,48},{80,64},{96,80},{112,96},{17,1},{33... | collective-permute-start | bytes 36872 | tf_op jit(solution)/shard_map/ppermute | solution.py:41
  377.1 59.1 %collective-permute-start.24 = (f32[3,1,8,128]{3,2,1,0:T(8,128)S(1)}, f32[3,1,8,128]{3,2,1,0:T(8,128)S(1)}, u32[]{:S(2)}, u32[]{:S(2)}) collective-permute-start(f32[3,1,8,128]{3,2,1,0:T(8,128)S(1)} %get-tuple-element.488), channel_id=1, source_target_pairs={{0,16},{16,32},{32,48},{48,64},{64,80},{80,96},{96,112},{1,17},{17... | collective-permute-start | bytes 36872 | tf_op jit(solution)/shard_map/ppermute | solution.py:40
  439.6 7.7 collective-permute-start.26
  458.4 7.7 collective-permute-start.30
  467.0 17.0 %collective-permute-start.31 = (f32[3,4,8,128]{3,2,1,0:T(8,128)S(1)}, f32[3,4,8,128]{3,2,1,0:T(8,128)S(1)}, u32[]{:S(2)}, u32[]{:S(2)}) collective-permute-start(f32[3,4,8,128]{3,2,1,0:T(8,128)S(1)} %fusion.65), channel_id=1, source_target_pairs={{0,1},{1,2},{2,3},{3,4},{4,5},{5,6},{6,7},{7,8},{8,9},{9,10},{10,1... | collective-permute-start | bytes 147464 | tf_op jit(solution)/shard_map/ppermute | solution.py:21
  467.1 19.2 %collective-permute-start.32 = (f32[3,4,8,128]{3,2,1,0:T(8,128)S(1)}, f32[3,4,8,128]{3,2,1,0:T(8,128)S(1)}, u32[]{:S(2)}, u32[]{:S(2)}) collective-permute-start(f32[3,4,8,128]{3,2,1,0:T(8,128)S(1)} %fusion.65), channel_id=1, source_target_pairs={{0,15},{1,0},{2,1},{3,2},{4,3},{5,4},{6,5},{7,6},{8,7},{9,8},{10,9... | collective-permute-start | bytes 147464 | tf_op jit(solution)/shard_map/ppermute | solution.py:26
  505.6 6.4 collective-permute-start.38
  520.6 6.7 collective-permute-start.41
  522.9 6.7 collective-permute-start.42
  531.7 6.6 collective-permute-start.44
  726.9 7.7 collective-permute-start.49
  800.1 6.5 collective-permute-start.52
  804.7 7.7 collective-permute-start.53
  821.6 7.7 collective-permute-start.57
  838.5 7.7 collective-permute-start.61
  (50 other events, 1303.3 us)
Sparse Core Ops, SparseCore 0:
  272.0 78.9 reduce-scatter.2
  717.9 70.5 reduce-scatter.4
